TPU v7x, 512 devices: a whole 4x8x8 slice. The times are simulated.
512 devices in a mesh: row: 8 (over y_lo, core), col: 64 (over z, y_hi, x).
Axes of the slice: x: 4, y: 8 (y_hi: 2, y_lo: 4; y = y_hi * 4 + y_lo), z: 8, core: 2. Of those that a mesh axis runs over, the one named last changes fastest.
Arguments:
- first_factor_strip: bfloat16 [4096, 8192], P('row', 'col'), may hold values from -16 to 16
- second_factor_strip: bfloat16 [8192, 24576], P('row', 'col'), may hold values from -0.0625 to 0.0625
- first_factor_support: int32 [32, 64], P('row', 'col'), may hold values 0 or 1
- second_factor_support: int32 [64, 192], P('row', 'col'), may hold values 0 or 1
- retained_blocks: int32 [32, 192], P('row', 'col'), may hold values 0 or 1
- target_bands: int32 [8, 64, 12, 1], P('row', 'col'), may hold values from 0 to 7; in each aligned block of 12 rows (0 to 11, 12 to 23, ..., all dimensions but the last counted through in order) at most 2 rows name the same one
Outputs:
- stochastic_result: bfloat16 [4096, 24576], P('row', 'col')
- redistributed_result: bfloat16 [16384, 8192], P('row', 'col')
Inputs may be any that keep to these rules, and one draw needn't show every extreme that they name: `target_bands`: among the tiles of one block no destination is named more than 2 times, and in some block one destination is named exactly 2 times.
All inputs are finite; a program needn't handle non-finite values. No bound on the sum of `first_factor_support` or of `second_factor_support` or of `retained_blocks` on one device may be relied on, other than what follows from the above.
Results may differ from a plain program's by a relative error of at most 0.001.
Values may be sent and summed in bfloat16 or wider, within the bound.
A program may use at most 64 MiB of HBM per device.

v0:
```python
import jax
import jax.numpy as jnp
from jax import lax
from jax.sharding import PartitionSpec as P

BLOCK_EDGE = 128


def squaring_pass(values, pattern):
    row_tiles, col_tiles = pattern.shape
    shaped = values.reshape(row_tiles, BLOCK_EDGE, col_tiles, BLOCK_EDGE)
    return (shaped * pattern[:, None, :, None].astype(values.dtype)).reshape(values.shape)


def body(
    first_factor_strip,
    second_factor_strip,
    first_factor_support,
    second_factor_support,
    retained_blocks,
    target_bands,
):
    a_eff = squaring_pass(first_factor_strip, first_factor_support)
    b_eff = squaring_pass(second_factor_strip, second_factor_support)
    a_whole = lax.all_gather(a_eff, "col", axis=1, tiled=True)
    multiplied_blocks = jnp.dot(
        a_whole,
        lax.all_gather(b_eff, "row", axis=0, tiled=True),
        preferred_element_type=jnp.float32,
    )
    powered_blocks = squaring_pass(multiplied_blocks * multiplied_blocks, retained_blocks)
    totals = lax.psum(jnp.sum(powered_blocks, axis=0), "row")
    block_bands = lax.axis_size("row")
    all_rows = powered_blocks.shape[0] * block_bands
    stochastic_result = (powered_blocks / (totals / all_rows + 1e-05)).astype(jnp.bfloat16)
    tile_rows = stochastic_result.shape[0] // BLOCK_EDGE
    tile_cols = stochastic_result.shape[1] // BLOCK_EDGE
    tile_count = tile_rows * tile_cols
    berth_limit = max(2, (tile_count + block_bands - 1) // block_bands)
    tile_stack = stochastic_result.reshape(tile_rows, BLOCK_EDGE, tile_cols, BLOCK_EDGE).transpose(
        0, 2, 1, 3
    )
    tile_stack = tile_stack.reshape(tile_count, BLOCK_EDGE * BLOCK_EDGE)
    targets = target_bands.reshape(tile_count)
    same_target = targets[:, None] == targets[None, :]
    earlier = jnp.arange(tile_count)[None, :] < jnp.arange(tile_count)[:, None]
    slot_rank = jnp.sum((same_target & earlier).astype(jnp.int32), axis=1)
    position = targets * berth_limit + slot_rank
    selector = (jnp.arange(block_bands * berth_limit)[:, None] == position[None, :]).astype(
        jnp.bfloat16
    )
    outgoing = jnp.dot(selector, tile_stack, preferred_element_type=jnp.float32).astype(
        jnp.bfloat16
    )
    outgoing = outgoing.reshape(block_bands, berth_limit, BLOCK_EDGE, BLOCK_EDGE)
    delivered_blocks = lax.all_to_all(outgoing, "row", split_axis=0, concat_axis=0, tiled=True)
    redistributed_result = delivered_blocks.reshape(
        block_bands * berth_limit * BLOCK_EDGE, BLOCK_EDGE
    )
    return (stochastic_result, redistributed_result)


def solution(mesh):
    placed = (
        P("row", "col"),
        P("row", "col"),
        P("row", "col"),
        P("row", "col"),
        P("row", "col"),
        P("row", "col", None, None),
    )
    return jax.shard_map(
        body,
        mesh=mesh,
        in_specs=placed,
        out_specs=(P("row", "col"), P("row", "col")),
        check_vma=False,
    )
```

profile of v0, /device:TPU:1, one launch (start us, length us, event | category | flops | bytes accessed | tf_op | source)
XLA Modules:
  0.0 290.4 jit_solution(5208302155169720494)
XLA Ops:
  7.2 0.7 convert_element_type.31
  7.9 1.4 copy.14
  9.3 0.2 mul.51
  9.5 1.0 bitcast_multiply_fusion
  10.6 0.7 convert_bitcast_fusion
  11.2 0.1 broadcast_bitcast_fusion
  11.3 1.7 broadcast_multiply_fusion
  13.0 0.7 convert_element_type.32
  13.7 0.1 copy.15
  13.8 0.2 mul.55
  14.1 0.3 copy.16
  14.3 0.2 convert_reduce_fusion
  14.5 76.6 %all-gather.5.cloned.1.call-done = bf16[8192,384]{0,1:T(8,128)(2,1)} async-done(((bf16[1024,384]{0,1:T(8,128)(2,1)}), bf16[8192,384]{0,1:T(8,128)(2,1)}) %all-gather.5.cloned.1.call-update) | async-done | bytes 6291472 | tf_op jit(solution)/shard_map/all_gather | solution.py:28
  91.1 147.4 %all-gather.3.cloned.1.call-done = bf16[512,8192]{1,0:T(8,128)(2,1)} async-done(((bf16[512,128]{1,0:T(8,128)(2,1)}), bf16[512,8192]{1,0:T(8,128)(2,1)}) %all-gather.3.cloned.1.call-update) | async-done | bytes 8388624 | tf_op jit(solution)/shard_map/all_gather | solution.py:25
  238.6 8.8 %fusion.4 = (f32[384]{0:T(512)S(1)}, f32[512,384]{1,0:T(8,128)S(1)}) fusion(f32[512,384]{1,0:T(8,128)S(1)} %copy.16, bf16[512,8192]{1,0:T(8,128)(2,1)} %all-gather.3.cloned.1.call-done, bf16[8192,384]{0,1:T(8,128)(2,1)} %all-gather.5.cloned.1.call-done), kind=kOutput, calls=%fused_computation.17 | convolution fusion | flops 3221814784 | bytes 16254464 | tf_op jit(solution)/shard_map/dot_general | solution.py:26
  247.4 16.6 %psum.7 = f32[384]{0:T(512)S(1)} all-reduce(f32[384]{0:T(512)S(1)} %get-tuple-element.2), channel_id=1, replica_groups=mesh['row'=8,'col'=64] {'row'}, use_global_device_ids=true, to_apply=%region_1.0 | all-reduce | flops 384 | bytes 3072 | tf_op jit(solution)/shard_map/psum | solution.py:32
  264.0 0.2 copy.17
  264.2 0.1 reshape.57
  264.3 0.3 copy.18
  264.7 0.3 copy.21
  265.1 0.3 fusion.1
  265.4 0.1 copy.22
  265.5 17.4 %all_to_all.5 = bf16[8,2,128,128]{3,2,1,0:T(8,128)(2,1)S(1)} all-to-all(bf16[8,2,128,128]{3,2,1,0:T(8,128)(2,1)S(1)} %bitcast.39), channel_id=1, replica_groups=mesh['row'=8,'col'=64] {'row'}, dimensions={0} | all-to-all | bytes 1048576 | tf_op jit(solution)/shard_map/all_to_all | solution.py:56
  282.8 0.8 copy.27
  (13 shorter events, 0.3 us)
Async XLA Ops:
  7.2 7.2 %copy-start.1 = (s32[1,1,12,1]{2,3,1,0:T(1,128)S(1)}, s32[1,1,12,1]{2,3,1,0:T(1,128)}, u32[]{:S(2)}) copy-start(s32[1,1,12,1]{2,3,1,0:T(1,128)} %param.11) | copy-start | bytes 148
  7.2 84.0 %all-gather.5.cloned.1.call-start = ((), (), s32[]{:S(2)}) async-start(), calls=%async_computation.2 | async-start | bytes 7077888 | tf_op jit(solution)/shard_map/all_gather | solution.py:28
  10.5 228.0 %all-gather.3.cloned.1.call-start = ((), (), s32[]{:S(2)}) async-start(), calls=%async_computation.1 | async-start | bytes 8519680 | tf_op jit(solution)/shard_map/all_gather | solution.py:25
  264.0 19.6 %copy-start = (bf16[512,384]{1,0:T(8,128)(2,1)}, bf16[512,384]{1,0:T(8,128)(2,1)S(1)}, u32[]{:S(2)}) copy-start(bf16[512,384]{1,0:T(8,128)(2,1)S(1)} %divide_convert_fusion) | copy-start | bytes 1179652
Sparse Core Ops, SparseCore 0:
  10.6 80.4 all-gather.4
  96.0 142.4 all-gather.2
where the time goes:
time: 291 us; the launch traced here: 290 us
  waiting for transfers between devices  224 us (77%)
  blocking collectives  33.9 us (12%)
  between operations  14.2 us (5%)
  matrix products  9.08 us (3%)
  other arithmetic  5 us (2%)
  local copies, waits for them, and re-layouts  4.13 us (1%)
    all_gather x1, waiting for transfers between devices, body(): a_whole = lax.all_gather(a_eff, 'col', axis=1, tiled=True)  147 us
    all_gather x1, waiting for transfers between devices, body(): lax.all_gather(b_eff, 'row', axis=0, tiled=True)  76.6 us
    all_to_all x1, blocking collectives, body(): lax.all_to_all(outgoing, 'row', split_axis=0, concat_axis=0, tiled=True)  17.4 us
    psum x1, blocking collectives, body(): totals = lax.psum(jnp.sum(powered_blocks, axis=0), 'row')  16.6 us
    dot_general x1, matrix products, body(): jnp.dot(a_whole, lax.all_gather(b_eff, 'row', axis=0, tiled=True), prefer...  8.81 us
  transfers between devices with their start and end apart: 2, of which 2 were waited for; matrix products, arithmetic and copies ran while one was open for 1% of the time, Pallas kernels for 0%

commit v1 on v0

v1 whole, which is shorter than its diff:
```python
import functools
import heapq

import jax
import jax.numpy as jnp
from jax import lax
from jax.experimental import pallas as pl
from jax.experimental.pallas import tpu as pltpu
from jax.sharding import PartitionSpec as P

MESH = pl.DeviceIdType.MESH
EDGE = 128
OWN, PARTNER = 0, 1
PARTS = {"full": (0, 512), "top": (0, 256), "bot": (256, 256)}
CHUNKS = ((0, 256), (256, 768))
PARTNER_READY = 13.0
BLOCK_US, HOP_US = 2.82, 1.8


def build_messages():
    msgs = []

    def add(axis, sign, dz, half, dx, part, level):
        came = (dz - sign, half, dx, part) if axis == "z" else (dz, half, dx - sign, part)
        msgs.append({"axis": axis, "sign": sign, "out": (dz, half, dx, part), "in": came, "level": level})

    for sign in (1, -1):
        add("x", sign, 0, OWN, 0, "full", 0)
    for sign in (1, -1):
        add("x", sign, 0, OWN, -sign, "top" if sign > 0 else "bot", 0)
    for dx in (0, -1, 1, 2):
        for step in range(4):
            for sign in (1, -1):
                part = "full" if step < 3 else ("top" if sign > 0 else "bot")
                add("z", sign, -sign * step, OWN, dx, part, 2)
    for step in range(4):
        for sign in (1, -1):
            part = "full" if step < 3 else ("top" if sign > 0 else "bot")
            add("z", sign, -sign * step, PARTNER, 0, part, 1)
    for dz in (0, -1, 1, -2, 2, -3, 3, 4):
        for sign in (1, -1):
            add("x", sign, dz, PARTNER, 0, "full", 1)
        for sign in (1, -1):
            add("x", sign, dz, PARTNER, -sign, "top" if sign > 0 else "bot", 1)
    return msgs


def halves(block):
    dz, half, dx, part = block
    key = (dz % 8, half, dx % 4)
    return {key + ("top",), key + ("bot",)} if part == "full" else {key + (part,)}


def plan(msgs):
    source = {}
    for k, m in enumerate(msgs):
        for h in halves(m["in"]):
            source[h] = k
    needs = [{source[h] for h in halves(m["out"]) if h in source} for m in msgs]
    ready_at = {}
    free = {("x", 1): 0.0, ("x", -1): 0.0, ("z", 1): 0.0, ("z", -1): 0.0}
    arrived, order, done = {}, [], set()
    heap = []
    for k, m in enumerate(msgs):
        if not needs[k]:
            heapq.heappush(heap, (PARTNER_READY if m["out"][1] == PARTNER else 0.0, m["level"], k))
    waited = set()
    events = []
    left = {k: set(n) for k, n in enumerate(needs)}
    partner_waited = False
    while heap:
        t, level, k = heapq.heappop(heap)
        m = msgs[k]
        link = (m["axis"], m["sign"])
        begin = max(t, free[link])
        size = PARTS[m["out"][3]][1] / 512 * BLOCK_US
        free[link] = begin + size
        arrived[k] = begin + size + HOP_US
        events.append((t, 1, k))
        for j, n in left.items():
            if k in n:
                n.discard(k)
                ready_at[j] = max(ready_at.get(j, 0.0), arrived[k])
                if not n:
                    heapq.heappush(heap, (ready_at[j], msgs[j]["level"], j))
    steps = []
    for t, _, k in events:
        for n in sorted(needs[k], key=lambda i: arrived[i]):
            if n not in waited:
                waited.add(n)
                steps.append((t, "wait", n))
        if msgs[k]["out"][1] == PARTNER and not partner_waited:
            partner_waited = True
            steps.append((t, "partner", 0))
        steps.append((t, "start", k))
    for k in sorted(arrived, key=lambda i: arrived[i]):
        if k not in waited:
            waited.add(k)
            steps.append((arrived[k], "wait", k))
    steps.sort(key=lambda s: s[0])
    return steps


def kernel(
    a_ref, b_ref, asup_ref, bsup_ref, keep_ref, band_ref,
    out_ref, moved_ref,
    a_all, b_all, acc, tiles, normal, outgoing, sums, slot_of, filled,
    a_send, a_recv, b_send, b_recv, s_send, s_recv, h_send, h_recv, c_send, c_recv, r_send, r_recv, local_sem,
):
    row, col = lax.axis_index("row"), lax.axis_index("col")
    y, core = row // 2, row % 2
    z, yh, x = col // 8, (col // 4) % 2, col % 4
    msgs = build_messages()
    steps = plan(msgs)

    def row_peer(k):
        py = (3 - y, (y + 2) % 4, y + 1 - 2 * (y % 2), y)[3 - k // 2]
        pc = 1 - core if k % 2 else core
        return py * 2 + pc

    def col_at(dz, dx, half):
        h = yh if half == OWN else 1 - yh
        return ((z + dz + 8) % 8) * 8 + h * 4 + (x + dx + 4) % 4

    across = ((y + 2) % 4) * 2 + core
    neighbours = [(row, col_at(0, 1, OWN)), (row, col_at(0, -1, OWN)), (row, col_at(1, 0, OWN)), (row, col_at(-1, 0, OWN))]
    neighbours += [(row_peer(k), col) for k in range(1, 8)]
    neighbours.append((across, col_at(0, 0, PARTNER)))

    barrier = pltpu.get_barrier_semaphore()
    for device in neighbours:
        pl.semaphore_signal(barrier, inc=1, device_id=device, device_id_type=MESH)

    for r in range(4):
        rows = pl.ds(r * EDGE, EDGE)
        tile = a_ref[rows, :]
        a_all[z, yh, x, rows, :] = jnp.where(asup_ref[r, 0] != 0, tile, jnp.zeros_like(tile))
    for r in range(8):
        for c in range(3):
            rows, cols = pl.ds(r * EDGE, EDGE), pl.ds(c * EDGE, EDGE)
            tile = b_ref[rows, cols]
            b_all[row, rows, cols] = jnp.where(bsup_ref[r, c] != 0, tile, jnp.zeros_like(tile))

    pl.semaphore_wait(barrier, len(neighbours))

    def block(spec):
        dz, half, dx, part = spec
        first, count = PARTS[part]
        h = yh if half == OWN else 1 - yh
        return a_all.at[(z + dz + 8) % 8, h, (x + dx + 4) % 4, pl.ds(first, count), :]

    def a_copy(k, spec):
        m = msgs[k]
        to = col_at(m["sign"], 0, OWN) if m["axis"] == "z" else col_at(0, m["sign"], OWN)
        return pltpu.make_async_remote_copy(
            src_ref=block(spec), dst_ref=block(spec), send_sem=a_send.at[k], recv_sem=a_recv.at[k],
            device_id=(row, to), device_id_type=MESH,
        )


    def half_copy(hop):
        if hop == 0:
            src, dst, to = a_all.at[z, yh, x], normal.at[:, pl.ds(0, EDGE)], (across, col)
        else:
            src, dst, to = normal.at[:, pl.ds(0, EDGE)], a_all.at[z, yh, x], (across, col_at(0, 0, PARTNER))
        return pltpu.make_async_remote_copy(
            src_ref=src, dst_ref=dst, send_sem=h_send.at[hop], recv_sem=h_recv.at[hop], device_id=to, device_id_type=MESH
        )

    def half_arrival():
        dst = a_all.at[z, 1 - yh, x]
        return pltpu.make_async_remote_copy(
            src_ref=dst, dst_ref=dst, send_sem=h_send.at[1], recv_sem=h_recv.at[1],
            device_id=(across, col_at(0, 0, PARTNER)), device_id_type=MESH,
        )

    def b_slab(py, pc, chunk):
        first, count = CHUNKS[chunk]
        return b_all.at[py * 2 + pc, pl.ds(first, count), :]

    def b_copy(sign, d, chunk, py):
        way = 0 if sign > 0 else 1
        return pltpu.make_async_remote_copy(
            src_ref=b_slab(py, core, chunk), dst_ref=b_slab(py, core, chunk),
            send_sem=b_send.at[way, d, chunk], recv_sem=b_recv.at[way, d, chunk],
            device_id=((y + sign) * 2 + core, col), device_id_type=MESH,
        )

    def sends(sign, d):
        return (y >= d) & (y <= 2) if sign > 0 else (y + d <= 3) & (y >= 1)

    def receives(sign, d):
        return y >= 1 + d if sign > 0 else y + 1 + d <= 3

    def relays(sign, d):
        return receives(sign, d) & (y <= 2 if sign > 0 else y >= 1)

    def ends(sign, d):
        return receives(sign, d) & (y == 3 if sign > 0 else y == 0)

    def sibling_copy(kind, chunk, py, pc):
        return pltpu.make_async_remote_copy(
            src_ref=b_slab(py, pc, chunk), dst_ref=b_slab(py, pc, chunk),
            send_sem=s_send.at[kind, chunk], recv_sem=s_recv.at[kind, chunk],
            device_id=(y * 2 + 1 - core, col), device_id_type=MESH,
        )

    def kind_of(sign, d):
        return 1 + d if sign > 0 else 4 + d

    def b_own(sign, chunk):
        @pl.when(sends(sign, 0))
        def _():
            b_copy(sign, 0, chunk, y).start()

    def b_arrival(sign, d, chunk, forward):
        @pl.when(relays(sign, d) if forward else ends(sign, d))
        def _():
            py = y - sign * (1 + d)
            b_copy(sign, d, chunk, py).wait_recv()
            if forward:
                b_copy(sign, d + 1, chunk, py).start()
            sibling_copy(kind_of(sign, d), chunk, py, core).start()

    half_copy(0).start()
    for k, m in enumerate(msgs):
        if m["out"] == (0, OWN, 0, "full"):
            a_copy(k, m["out"]).start()
    for sign in (1, -1):
        b_own(sign, 0)
    half_copy(0).wait_recv()
    half_copy(1).start()
    for sign in (1, -1):
        b_own(sign, 1)
    for chunk in range(2):
        sibling_copy(0, chunk, y, core).start()

    bands = [band_ref[0, 0, t, 0] for t in range(12)]
    places = []
    for t in range(12):
        rank = jnp.int32(0)
        for u in range(t):
            rank = rank + jnp.where(bands[u] == bands[t], 1, 0)
        places.append(bands[t] * 2 + rank)
    for p in range(16):
        which, any_of = jnp.int32(0), jnp.int32(0)
        for t in range(12):
            hit = places[t] == p
            which = jnp.where(hit, t, which)
            any_of = jnp.where(hit, 1, any_of)
        slot_of[p] = which
        filled[p] = any_of

    extra = []
    for d in range(2):
        for chunk, late in ((0, 12.5), (1, 25.5)):
            for sign in (1, -1):
                extra.append((17.0 * d + late, functools.partial(b_arrival, sign, d, chunk, True)))
    for d, late in ((0, 33.0), (1, 46.0)):
        for chunk in range(2):
            for sign in (1, -1):
                extra.append((late, functools.partial(b_arrival, sign, d, chunk, False)))
    extra.sort(key=lambda e: e[0])
    for t, what, k in steps:
        while extra and extra[0][0] <= t:
            extra.pop(0)[1]()
        if what == "wait":
            a_copy(k, msgs[k]["in"]).wait_recv()
        elif what == "partner":
            half_arrival().wait_recv()
        elif msgs[k]["out"] != (0, OWN, 0, "full"):
            a_copy(k, msgs[k]["out"]).start()
    for _, act in extra:
        act()

    def sibling_arrived(kind, py):
        for chunk in range(2):
            sibling_copy(kind, chunk, py, 1 - core).wait_recv()

    sibling_arrived(0, y)
    for d in range(2):
        for sign in (1, -1):
            @pl.when(receives(sign, d))
            def _():
                sibling_arrived(kind_of(sign, d), y - sign * (1 + d))

    def multiply(i):
        near = i // 2
        py = jnp.where(y < 2, near, 3 - near)
        slab = py * 2 + i % 2
        left = jnp.concatenate([a_all[slab, h, k] for h in range(2) for k in range(4)], axis=1)
        return jnp.dot(left, b_all[slab], preferred_element_type=jnp.float32)

    acc[...] = jnp.zeros_like(acc)

    def more(i, carry):
        acc[...] += multiply(i)
        return carry

    lax.fori_loop(0, 6, more, 0)
    for chunk in range(2):
        for sign in (1, -1):
            b_arrival(sign, 2, chunk, False)
    for sign in (1, -1):
        @pl.when(receives(sign, 2))
        def _():
            sibling_arrived(kind_of(sign, 2), y - sign * 3)
    lax.fori_loop(6, 8, more, 0)

    for c in range(3):
        cols = pl.ds(c * EDGE, EDGE)
        total = jnp.zeros((1, EDGE), jnp.float32)
        for r in range(4):
            rows = pl.ds(r * EDGE, EDGE)
            tile = acc[rows, cols]
            tile = jnp.where(keep_ref[r, c] != 0, tile * tile, jnp.zeros_like(tile))
            acc[rows, cols] = tile
            total = total + jnp.sum(tile, axis=0, keepdims=True)
        sums[row, :, cols] = total

    def sum_copy(k, who):
        return pltpu.make_async_remote_copy(
            src_ref=sums.at[who], dst_ref=sums.at[who], send_sem=c_send.at[k], recv_sem=c_recv.at[k],
            device_id=(row_peer(k), col), device_id_type=MESH,
        )

    for k in range(7, 0, -1):
        sum_copy(k, row).start()
    for k in range(7, 0, -1):
        sum_copy(k, row_peer(k)).wait_recv()

    half_copy(1).wait_send()
    total = sums[0]
    for i in range(1, 8):
        total = total + sums[i]
    scale = 1.0 / (total / (8 * 512) + 1e-5)
    for r in range(4):
        for c in range(3):
            rows, cols = pl.ds(r * EDGE, EDGE), pl.ds(c * EDGE, EDGE)
            tile = (acc[rows, cols] * scale[:, c * EDGE:(c + 1) * EDGE]).astype(jnp.bfloat16)
            normal[rows, cols] = tile
            tiles[r * 3 + c] = tile

    for p in range(16):
        tile = tiles[slot_of[p]]
        outgoing[p // 2, p % 2] = jnp.where(filled[p] != 0, tile, jnp.zeros_like(tile))

    def move(k, who):
        return pltpu.make_async_remote_copy(
            src_ref=outgoing.at[row_peer(k)], dst_ref=moved_ref.at[who], send_sem=r_send.at[k], recv_sem=r_recv.at[k],
            device_id=(row_peer(k), col), device_id_type=MESH,
        )

    for k in range(7, 0, -1):
        move(k, row).start()
    keep = pltpu.make_async_copy(outgoing.at[row], moved_ref.at[row], local_sem.at[0])
    keep.start()
    result = pltpu.make_async_copy(normal, out_ref, local_sem.at[1])
    result.start()

    half_copy(0).wait_send()
    for k, m in enumerate(msgs):
        a_copy(k, m["out"]).wait_send()
    for d in range(3):
        for sign in (1, -1):
            @pl.when(sends(sign, d))
            def _():
                for chunk in range(2):
                    b_copy(sign, d, chunk, y - sign * d).wait_send()

            @pl.when(receives(sign, d))
            def _():
                for chunk in range(2):
                    sibling_copy(kind_of(sign, d), chunk, y - sign * (1 + d), core).wait_send()
    for chunk in range(2):
        sibling_copy(0, chunk, y, core).wait_send()
    for k in range(7, 0, -1):
        sum_copy(k, row).wait_send()
    keep.wait()
    result.wait()
    for k in range(7, 0, -1):
        move(k, row).wait_send()
        move(k, row_peer(k)).wait_recv()


def body(a, b, a_support, b_support, keep, bands):
    count = len(build_messages())
    dma = pltpu.SemaphoreType.DMA
    vmem, smem = pl.BlockSpec(memory_space=pltpu.VMEM), pl.BlockSpec(memory_space=pltpu.SMEM)
    anywhere = pl.BlockSpec(memory_space=pl.ANY)
    out, moved = pl.pallas_call(
        kernel,
        out_shape=(
            jax.ShapeDtypeStruct((512, 384), jnp.bfloat16),
            jax.ShapeDtypeStruct((8, 2, EDGE, EDGE), jnp.bfloat16),
        ),
        in_specs=[vmem, vmem, smem, smem, smem, smem],
        out_specs=(anywhere, anywhere),
        scratch_shapes=[
            pltpu.VMEM((8, 2, 4, 512, EDGE), jnp.bfloat16),
            pltpu.VMEM((8, 1024, 384), jnp.bfloat16),
            pltpu.VMEM((512, 384), jnp.float32),
            pltpu.VMEM((12, EDGE, EDGE), jnp.bfloat16),
            pltpu.VMEM((512, 384), jnp.bfloat16),
            pltpu.VMEM((8, 2, EDGE, EDGE), jnp.bfloat16),
            pltpu.VMEM((8, 1, 384), jnp.float32),
            pltpu.SMEM((16,), jnp.int32),
            pltpu.SMEM((16,), jnp.int32),
            dma((count,)), dma((count,)),
            dma((2, 3, 2)), dma((2, 3, 2)),
            dma((7, 2)), dma((7, 2)),
            dma((2,)), dma((2,)),
            dma((8,)), dma((8,)),
            dma((8,)), dma((8,)),
            dma((2,)),
        ],
        compiler_params=pltpu.CompilerParams(
            collective_id=0, has_side_effects=True, vmem_limit_bytes=40 * 1024 * 1024
        ),
        name="expand_and_move",
    )(a, b, a_support, b_support, keep, bands)
    return out, moved.reshape(2048, EDGE)


def solution(mesh):
    split = P("row", "col")
    return jax.shard_map(
        body,
        mesh=mesh,
        in_specs=(split, split, split, split, split, P("row", "col", None, None)),
        out_specs=(split, split),
        check_vma=False,
    )
```

time: 291 us -> 116 us (0.40)
  waiting for transfers between devices: 224 us -> 0 us
  Pallas kernels: 0 us -> 110 us
  blocking collectives: 33.9 us -> 0 us
  between operations: 14.2 us -> 0.65 us
  matrix products: 9.08 us -> 0 us
  other arithmetic: 5 us -> 0 us
    all_gather x2 -> x0, waiting for transfers between devices: 224 us -> none  [the longest x1 147 us: body(): a_whole = lax.all_gather(a_eff, 'col', axis=1, tiled=True)]
    pallas_call x0 -> x1, Pallas kernels: none -> 110 us  [body(): pl.pallas_call(kernel, out_shape=(jax.ShapeDtypeStruct((512, 384), jnp.bf...]
    all_to_all x1 -> x0, blocking collectives: 17.4 us -> none  [body(): lax.all_to_all(outgoing, 'row', split_axis=0, concat_axis=0, tiled=True)]
    psum x1 -> x0, blocking collectives: 16.6 us -> none  [body(): totals = lax.psum(jnp.sum(powered_blocks, axis=0), 'row')]
    dot_general x2 -> x0, matrix products: 9.08 us -> none  [the longest x1 8.81 us: body(): jnp.dot(a_whole, lax.all_gather(b_eff, 'row', axis=0, tiled=True), prefer...]
    unnamed x10 -> x15, local copies, waits for them, and re-layouts: 2.75 us -> 5.66 us
  transfers between devices with their start and end apart: 2 -> 0, of which waited for: 2 -> 0; matrix products, arithmetic and copies ran while one was open for 1% -> 0% of each run, Pallas kernels for 0% -> 0%
where the time goes in v1:
time: 116 us
  Pallas kernels  110 us (95%)
  local copies, waits for them, and re-layouts  5.66 us (5%)
    pallas_call x1, Pallas kernels, body(): pl.pallas_call(kernel, out_shape=(jax.ShapeDtypeStruct((512, 384), jnp.bf...  110 us
    unnamed x15, local copies, waits for them, and re-layouts  5.66 us

profile of v1, /device:TPU:1, one launch (start us, length us, event | category | flops | bytes accessed | tf_op | source)
XLA Modules:
  0.0 116.0 jit_solution(11697387849981153742)
XLA Ops:
  0.6 0.0 copy-start.3
  0.6 0.7 copy.8.asup_ref
  1.4 0.0 copy-done.3
  1.4 0.0 copy-start.4
  1.4 0.1 copy.9.bsup_ref
  1.5 0.6 copy-done.4
  2.0 0.0 copy-start.2
  2.0 0.1 copy.10.band_ref
  2.1 0.6 copy-done.2
  2.7 0.0 copy-start
  2.7 1.1 copy-done
  3.9 0.0 copy-start.1
  3.9 0.9 copy-done.1
  4.8 109.7 %expand_and_move.1 = (bf16[512,384]{1,0:T(8,128)(2,1)S(1)}, bf16[8,2,128,128]{3,2,1,0:T(8,128)(2,1)S(1)}) custom-call(bf16[512,128]{1,0:T(8,128)(2,1)S(1)} %copy-done.1, bf16[1024,384]{1,0:T(8,128)(2,1)S(1)} %copy-done, s32[4,1]{1,0:T(4,128)S(1)} %copy.8.asup_ref, s32[8,3]{1,0:T(8,128)S(1)} %copy.9.bsup_ref, s32[4,3]{1,0:T(4,128)S(1)} %copy-done.2, ...), custom_call_target="tpu_custom_call" | custom-call | tf_op jit(solution)/shard_map/expand_and_move/pallas_call | solution.py:391
  114.5 0.7 copy.13
  115.2 0.8 copy.14
Async XLA Ops:
  0.6 0.8 copy-start.3
  1.4 0.7 copy-start.4
  2.0 0.7 copy-start.2
  2.7 1.1 copy-start
  3.9 0.9 copy-start.1

commit v2 on v1

v2 whole, which is shorter than its diff:
```python
import functools
import heapq

import jax
import jax.numpy as jnp
from jax import lax
from jax.experimental import pallas as pl
from jax.experimental.pallas import tpu as pltpu
from jax.sharding import PartitionSpec as P

MESH = pl.DeviceIdType.MESH
EDGE = 128
OWN, PARTNER = 0, 1
PARTS = {"full": (0, 512), "top": (0, 256), "bot": (256, 256)}
CHUNKS = ((0, 256), (256, 768))
PARTNER_READY = 12.0
BLOCK_US, HOP_US = 2.82, 1.8


def build_messages():
    msgs = []

    def add(axis, sign, dz, half, dx, part, level):
        came = (dz - sign, half, dx, part) if axis == "z" else (dz, half, dx - sign, part)
        msgs.append({"axis": axis, "sign": sign, "out": (dz, half, dx, part), "in": came, "level": level})

    for sign in (1, -1):
        add("x", sign, 0, OWN, 0, "full", 0)
    for sign in (1, -1):
        add("x", sign, 0, OWN, -sign, "top" if sign > 0 else "bot", 0)
    for dx in (0, -1, 1, 2):
        for step in range(4):
            for sign in (1, -1):
                part = "full" if step < 3 else ("top" if sign > 0 else "bot")
                add("z", sign, -sign * step, OWN, dx, part, 2 + step)
    for step in range(4):
        for sign in (1, -1):
            part = "full" if step < 3 else ("top" if sign > 0 else "bot")
            add("z", sign, -sign * step, PARTNER, 0, part, 1)
    for dz in (0, -1, 1, -2, 2, -3, 3, 4):
        for sign in (1, -1):
            add("x", sign, dz, PARTNER, 0, "full", 1)
        for sign in (1, -1):
            add("x", sign, dz, PARTNER, -sign, "top" if sign > 0 else "bot", 1)
    return msgs


def halves(block):
    dz, half, dx, part = block
    key = (dz % 8, half, dx % 4)
    return {key + ("top",), key + ("bot",)} if part == "full" else {key + (part,)}


def plan(msgs):
    source = {}
    for k, m in enumerate(msgs):
        for h in halves(m["in"]):
            source[h] = k
    needs = [{source[h] for h in halves(m["out"]) if h in source} for m in msgs]
    left = [set(n) for n in needs]
    links = [("x", 1), ("x", -1), ("z", 1), ("z", -1)]
    busy = {link: 0.0 for link in links}
    waiting = {link: [] for link in links}
    issued = {link: 0.0 for link in links}
    ready, arrived, starts = {}, {}, []
    events = []
    for k, m in enumerate(msgs):
        if not needs[k]:
            heapq.heappush(events, (PARTNER_READY if m["out"][1] == PARTNER else 0.0, 0, k))
    while events:
        t, kind, k = heapq.heappop(events)
        touched = links
        if kind == 0:
            m = msgs[k]
            ready[k] = t
            touched = [(m["axis"], m["sign"])]
            heapq.heappush(waiting[touched[0]], (m["level"], k))
        elif kind == 2:
            for n, rest in enumerate(left):
                if k in rest:
                    rest.discard(k)
                    if not rest:
                        heapq.heappush(events, (t, 0, n))
        for link in touched:
            if busy[link] <= t and waiting[link]:
                n = heapq.heappop(waiting[link])[1]
                busy[link] = t + PARTS[msgs[n]["out"][3]][1] / 512 * BLOCK_US
                arrived[n] = busy[link] + HOP_US
                issued[link] = max(issued[link], ready[n])
                starts.append((issued[link], n))
                heapq.heappush(events, (busy[link], 1, n))
                heapq.heappush(events, (arrived[n], 2, n))
    starts.sort(key=lambda e: e[0])
    relayed = set().union(*needs)
    waited = set()
    steps = []
    for t, k in starts:
        for n in sorted(needs[k], key=lambda i: arrived[i]):
            if n not in waited:
                waited.add(n)
                steps.append((t, "wait", n))
        if msgs[k]["out"][1] == PARTNER and "partner" not in waited:
            waited.add("partner")
            steps.append((t, "partner", 0))
        steps.append((t, "start", k))
    groups = {}
    for k, m in enumerate(msgs):
        if k not in relayed:
            groups.setdefault((m["in"][0] % 8, m["in"][1]), []).append(k)
    for g, members in groups.items():
        steps.append((max(arrived[k] for k in members), "group", g))
    steps.sort(key=lambda e: e[0])
    return steps, sorted(groups), relayed


def kernel(
    a_hbm, b_hbm, asup_hbm, bsup_hbm, keep_hbm, band_hbm,
    out_ref, moved_ref,
    a_all, b_all, acc, tiles, outgoing, sums, relay, a_in, b_in,
    asup_ref, bsup_ref, keep_ref, band_ref, slot_of, filled,
    a_send, a_recv, g_recv, b_send, b_recv, s_send, s_recv, h_recv, c_send, c_recv, r_send, r_recv, local_sem,
):
    row, col = lax.axis_index("row"), lax.axis_index("col")
    y, core = row // 2, row % 2
    z, yh, x = col // 8, (col // 4) % 2, col % 4
    msgs = build_messages()
    steps, groups, relayed = plan(msgs)

    def row_peer(k):
        py = (3 - y, (y + 2) % 4, y + 1 - 2 * (y % 2), y)[3 - k // 2]
        pc = 1 - core if k % 2 else core
        return py * 2 + pc

    def col_at(dz, dx, half):
        h = yh if half == OWN else 1 - yh
        return ((z + dz + 8) % 8) * 8 + h * 4 + (x + dx + 4) % 4

    across = ((y + 2) % 4) * 2 + core
    neighbours = [(row, col_at(0, 1, OWN)), (row, col_at(0, -1, OWN)), (row, col_at(1, 0, OWN)), (row, col_at(-1, 0, OWN))]
    neighbours += [(row_peer(k), col) for k in range(1, 8)]
    neighbours.append((across, col_at(0, 0, PARTNER)))

    barrier = pltpu.get_barrier_semaphore()
    for device in neighbours:
        pl.semaphore_signal(barrier, inc=1, device_id=device, device_id_type=MESH)

    loads = [
        pltpu.make_async_copy(src, dst, local_sem.at[k])
        for k, (src, dst) in enumerate(
            ((asup_hbm, asup_ref), (a_hbm, a_in), (bsup_hbm, bsup_ref), (b_hbm, b_in), (keep_hbm, keep_ref), (band_hbm, band_ref))
        )
    ]
    for load in loads:
        load.start()

    loads[0].wait()
    loads[1].wait()
    for r in range(4):
        rows = pl.ds(r * EDGE, EDGE)
        tile = a_in[rows, :]
        a_all[z, yh, x, rows, :] = jnp.where(asup_ref[0, r] != 0, tile, jnp.zeros_like(tile))

    pl.semaphore_wait(barrier, len(neighbours))

    def block(spec):
        dz, half, dx, part = spec
        first, count = PARTS[part]
        h = yh if half == OWN else 1 - yh
        return a_all.at[(z + dz + 8) % 8, h, (x + dx + 4) % 4, pl.ds(first, count), :]

    def a_copy(k, spec):
        m = msgs[k]
        to = col_at(m["sign"], 0, OWN) if m["axis"] == "z" else col_at(0, m["sign"], OWN)
        return pltpu.make_async_remote_copy(
            src_ref=block(spec), dst_ref=block(spec), send_sem=a_send.at[0], recv_sem=a_recv.at[k] if k in relayed else g_recv.at[groups.index((m["in"][0] % 8, m["in"][1]))],
            device_id=(row, to), device_id_type=MESH,
        )

    def group_arrived(g):
        dz, half = g
        ref = a_all.at[(z + dz) % 8, yh] if half == OWN else a_all.at[(z + dz) % 8, 1 - yh, (x + 2) % 4]
        pltpu.make_async_remote_copy(
            src_ref=ref, dst_ref=ref, send_sem=a_send.at[0], recv_sem=g_recv.at[groups.index(g)],
            device_id=(row, col_at(1, 0, OWN)), device_id_type=MESH,
        ).wait_recv()

    def half_copy(hop):
        if hop == 0:
            src, dst, to = a_all.at[z, yh, x], relay, (across, col)
        else:
            src, dst, to = relay, a_all.at[z, yh, x], (across, col_at(0, 0, PARTNER))
        return pltpu.make_async_remote_copy(
            src_ref=src, dst_ref=dst, send_sem=a_send.at[0], recv_sem=h_recv.at[hop], device_id=to, device_id_type=MESH
        )

    def half_arrival():
        dst = a_all.at[z, 1 - yh, x]
        return pltpu.make_async_remote_copy(
            src_ref=dst, dst_ref=dst, send_sem=a_send.at[0], recv_sem=h_recv.at[1],
            device_id=(across, col_at(0, 0, PARTNER)), device_id_type=MESH,
        )

    def b_slab(py, pc, chunk):
        first, count = CHUNKS[chunk]
        return b_all.at[py * 2 + pc, pl.ds(first, count), :]

    def b_copy(sign, d, chunk, py):
        way = 0 if sign > 0 else 1
        return pltpu.make_async_remote_copy(
            src_ref=b_slab(py, core, chunk), dst_ref=b_slab(py, core, chunk),
            send_sem=b_send.at[0], recv_sem=b_recv.at[way, d, chunk],
            device_id=((y + sign) * 2 + core, col), device_id_type=MESH,
        )

    def sends(sign, d):
        return (y >= d) & (y <= 2) if sign > 0 else (y + d <= 3) & (y >= 1)

    def receives(sign, d):
        return y >= 1 + d if sign > 0 else y + 1 + d <= 3

    def relays(sign, d):
        return receives(sign, d) & (y <= 2 if sign > 0 else y >= 1)

    def ends(sign, d):
        return receives(sign, d) & (y == 3 if sign > 0 else y == 0)

    def sibling_copy(kind, chunk, py, pc):
        return pltpu.make_async_remote_copy(
            src_ref=b_slab(py, pc, chunk), dst_ref=b_slab(py, pc, chunk),
            send_sem=s_send.at[0], recv_sem=s_recv.at[1 if kind in (3, 6) else 0],
            device_id=(y * 2 + 1 - core, col), device_id_type=MESH,
        )

    def kind_of(sign, d):
        return 1 + d if sign > 0 else 4 + d

    def b_own(sign, chunk):
        @pl.when(sends(sign, 0))
        def _():
            b_copy(sign, 0, chunk, y).start()

    def b_arrival(sign, d, chunk, forward):
        @pl.when(relays(sign, d) if forward else ends(sign, d))
        def _():
            py = y - sign * (1 + d)
            b_copy(sign, d, chunk, py).wait_recv()
            if forward:
                b_copy(sign, d + 1, chunk, py).start()
            sibling_copy(kind_of(sign, d), chunk, py, core).start()

    half_copy(0).start()
    for k, m in enumerate(msgs):
        if m["out"] == (0, OWN, 0, "full"):
            a_copy(k, m["out"]).start()
    loads[2].wait()
    loads[3].wait()
    for r in range(8):
        for c in range(3):
            rows, cols = pl.ds(r * EDGE, EDGE), pl.ds(c * EDGE, EDGE)
            tile = b_in[rows, cols]
            b_all[row, rows, cols] = jnp.where(bsup_ref[c, r] != 0, tile, jnp.zeros_like(tile))
    for sign in (1, -1):
        b_own(sign, 0)
    half_copy(0).wait_recv()
    half_copy(1).start()
    for sign in (1, -1):
        b_own(sign, 1)
    for chunk in range(2):
        sibling_copy(0, chunk, y, core).start()
    loads[4].wait()
    loads[5].wait()

    bands = [band_ref[0, t] for t in range(12)]
    places = []
    for t in range(12):
        rank = jnp.int32(0)
        for u in range(t):
            rank = rank + jnp.where(bands[u] == bands[t], 1, 0)
        places.append(bands[t] * 2 + rank)
    for p in range(16):
        which, any_of = jnp.int32(0), jnp.int32(0)
        for t in range(12):
            hit = places[t] == p
            which = jnp.where(hit, t, which)
            any_of = jnp.where(hit, 1, any_of)
        slot_of[p] = which
        filled[p] = any_of

    far = jnp.where(y == 0, 3, jnp.where(y == 3, 0, -1))

    def multiply(slab):
        left = jnp.concatenate([a_all[slab, h, k] for h in range(2) for k in range(4)], axis=1)
        acc[...] += jnp.dot(left, b_all[slab], preferred_element_type=jnp.float32)

    def early(dz):
        slab = (z + dz + 8) % 8

        @pl.when(slab // 2 != far)
        def _():
            multiply(slab)

    def siblings_arrived(count, late):
        ref = b_all.at[pl.ds(0, count)]
        pltpu.make_async_remote_copy(
            src_ref=ref, dst_ref=ref, send_sem=s_send.at[0], recv_sem=s_recv.at[late],
            device_id=(y * 2 + 1 - core, col), device_id_type=MESH,
        ).wait_recv()

    def early_siblings():
        pl.when(far >= 0)(lambda: siblings_arrived(3, 0))
        pl.when(far < 0)(lambda: siblings_arrived(4, 0))

    acc[...] = jnp.zeros_like(acc)

    extra = []
    for d in range(2):
        for chunk, late in ((0, 12.5), (1, 25.5)):
            for sign in (1, -1):
                extra.append((17.0 * d + late, functools.partial(b_arrival, sign, d, chunk, True)))
    for d, late in ((0, 33.0), (1, 43.5)):
        for chunk in range(2):
            for sign in (1, -1):
                extra.append((late, functools.partial(b_arrival, sign, d, chunk, False)))
    extra.append((45.5, early_siblings))
    for late, dz in ((46.0, 0), (47.0, -1), (48.0, 1), (49.0, -2), (50.0, 2), (51.0, -3), (52.0, 3), (99.0, 4)):
        extra.append((late, functools.partial(early, dz)))
    extra.sort(key=lambda e: e[0])
    for t, what, k in steps:
        while extra and extra[0][0] <= t:
            extra.pop(0)[1]()
        if what == "wait":
            a_copy(k, msgs[k]["in"]).wait_recv()
        elif what == "group":
            group_arrived(k)
        elif what == "partner":
            half_arrival().wait_recv()
        elif msgs[k]["out"] != (0, OWN, 0, "full") or msgs[k]["axis"] == "z" and False:
            a_copy(k, msgs[k]["out"]).start()
    for _, act in extra:
        act()

    for chunk in range(2):
        for sign in (1, -1):
            b_arrival(sign, 2, chunk, False)

    @pl.when(far >= 0)
    def _():
        def more(i, carry):
            @pl.when(i == 1)
            def _():
                siblings_arrived(1, 1)

            multiply(far * 2 + (core + i) % 2)
            return carry

        lax.fori_loop(0, 2, more, 0)

    for c in range(3):
        cols = pl.ds(c * EDGE, EDGE)
        total = jnp.zeros((1, EDGE), jnp.float32)
        for r in range(4):
            rows = pl.ds(r * EDGE, EDGE)
            tile = acc[rows, cols]
            tile = jnp.where(keep_ref[r, c] != 0, tile * tile, jnp.zeros_like(tile))
            acc[rows, cols] = tile
            total = total + jnp.sum(tile, axis=0, keepdims=True)
        sums[row, :, cols] = total

    def sum_copy(k, who):
        return pltpu.make_async_remote_copy(
            src_ref=sums.at[who], dst_ref=sums.at[who], send_sem=c_send.at[0], recv_sem=c_recv.at[0],
            device_id=(row_peer(k), col), device_id_type=MESH,
        )

    for k in range(7, 0, -1):
        sum_copy(k, row).start()
    all_sums = pltpu.make_async_remote_copy(
        src_ref=sums.at[pl.ds(0, 7)], dst_ref=sums.at[pl.ds(0, 7)], send_sem=c_send.at[0], recv_sem=c_recv.at[0],
        device_id=(row_peer(1), col), device_id_type=MESH,
    )
    all_sums.wait_recv()

    total = sums[0]
    for i in range(1, 8):
        total = total + sums[i]
    scale = 1.0 / (total / (8 * 512) + 1e-5)
    for r in range(4):
        for c in range(3):
            rows, cols = pl.ds(r * EDGE, EDGE), pl.ds(c * EDGE, EDGE)
            tile = (acc[rows, cols] * scale[:, c * EDGE:(c + 1) * EDGE]).astype(jnp.bfloat16)
            out_ref[rows, cols] = tile
            tiles[r * 3 + c] = tile

    for p in range(16):
        tile = tiles[slot_of[p]]
        outgoing[p // 2, p % 2] = jnp.where(filled[p] != 0, tile, jnp.zeros_like(tile))

    def move(k, who):
        return pltpu.make_async_remote_copy(
            src_ref=outgoing.at[row_peer(k)], dst_ref=moved_ref.at[who], send_sem=r_send.at[0], recv_sem=r_recv.at[0],
            device_id=(row_peer(k), col), device_id_type=MESH,
        )

    for k in range(7, 0, -1):
        move(k, row).start()
    moved_ref[row] = outgoing[row]

    def sent(ref, sem):
        pltpu.make_async_remote_copy(
            src_ref=ref, dst_ref=ref, send_sem=sem.at[0], recv_sem=r_recv.at[0], device_id=(row_peer(1), col), device_id_type=MESH
        ).wait_send()

    sent(a_all, a_send)
    pl.when(far >= 0)(lambda: sent(b_all.at[pl.ds(0, 1)], b_send))
    pl.when(far < 0)(lambda: sent(b_all.at[pl.ds(0, 5)], b_send))
    sent(b_all.at[pl.ds(0, 4)], s_send)
    all_sums.wait_send()
    every = pltpu.make_async_remote_copy(
        src_ref=outgoing.at[pl.ds(0, 7)], dst_ref=moved_ref.at[pl.ds(0, 7)], send_sem=r_send.at[0], recv_sem=r_recv.at[0],
        device_id=(row_peer(1), col), device_id_type=MESH,
    )
    every.wait_send()
    every.wait_recv()


def body(a, b, a_support, b_support, keep, bands):
    count = len(build_messages())
    dma = pltpu.SemaphoreType.DMA
    there = pl.BlockSpec(memory_space=pltpu.HBM)
    vmem = pl.BlockSpec(memory_space=pltpu.VMEM)
    out, moved = pl.pallas_call(
        kernel,
        out_shape=(
            jax.ShapeDtypeStruct((512, 384), jnp.bfloat16),
            jax.ShapeDtypeStruct((8, 2, EDGE, EDGE), jnp.bfloat16),
        ),
        in_specs=[there] * 6,
        out_specs=(vmem, vmem),
        scratch_shapes=[
            pltpu.VMEM((8, 2, 4, 512, EDGE), jnp.bfloat16),
            pltpu.VMEM((8, 1024, 384), jnp.bfloat16),
            pltpu.VMEM((512, 384), jnp.float32),
            pltpu.VMEM((12, EDGE, EDGE), jnp.bfloat16),
            pltpu.VMEM((8, 2, EDGE, EDGE), jnp.bfloat16),
            pltpu.VMEM((8, 1, 384), jnp.float32),
            pltpu.VMEM((512, EDGE), jnp.bfloat16),
            pltpu.VMEM((512, EDGE), jnp.bfloat16),
            pltpu.VMEM((1024, 384), jnp.bfloat16),
            pltpu.SMEM((1, 4), jnp.int32),
            pltpu.SMEM((3, 8), jnp.int32),
            pltpu.SMEM((4, 3), jnp.int32),
            pltpu.SMEM((1, 12), jnp.int32),
            pltpu.SMEM((16,), jnp.int32),
            pltpu.SMEM((16,), jnp.int32),
            dma((1,)), dma((count,)), dma((9,)),
            dma((1,)), dma((2, 3, 2)),
            dma((1,)), dma((2,)),
            dma((2,)),
            dma((1,)), dma((1,)),
            dma((1,)), dma((1,)),
            dma((6,)),
        ],
        compiler_params=pltpu.CompilerParams(
            collective_id=0, has_side_effects=True, vmem_limit_bytes=67043328
        ),
        name="expand_and_move",
    )(a, b, a_support.T, b_support.T, keep, bands.reshape(1, 12))
    return out, moved.reshape(2048, EDGE)


def solution(mesh):
    split = P("row", "col")
    return jax.shard_map(
        body,
        mesh=mesh,
        in_specs=(split, split, split, split, split, P("row", "col", None, None)),
        out_specs=(split, split),
        check_vma=False,
    )
```

time: 116 us -> 96.6 us (0.83)
  Pallas kernels: 110 us -> 93.1 us
  local copies, waits for them, and re-layouts: 5.66 us -> 2.64 us
    pallas_call x1, Pallas kernels: 110 us -> 93.1 us  [body(): pl.pallas_call(kernel, out_shape=(jax.ShapeDtypeStruct((512, 384), jnp.bf...]
    unnamed x15 -> x4, local copies, waits for them, and re-layouts: 5.66 us -> 2.64 us
where the time goes in v2:
time: 96.6 us; the launch traced here: 96.4 us
  Pallas kernels  93.1 us (96%)
  local copies, waits for them, and re-layouts  2.64 us (3%)
    pallas_call x1, Pallas kernels, body(): pl.pallas_call(kernel, out_shape=(jax.ShapeDtypeStruct((512, 384), jnp.bf...  93.1 us
    unnamed x4, local copies, waits for them, and re-layouts  2.64 us

profile of v2, /device:TPU:1, one launch (start us, length us, event | category | flops | bytes accessed | tf_op | source)
XLA Modules:
  0.0 96.4 jit_solution(9129666373428762980)
XLA Ops:
  0.6 93.1 %expand_and_move.1 = (bf16[512,384]{1,0:T(8,128)(2,1)}, bf16[8,2,128,128]{3,2,1,0:T(8,128)(2,1)}) custom-call(bf16[512,128]{1,0:T(8,128)(2,1)} %a_hbm.1, bf16[1024,384]{1,0:T(8,128)(2,1)} %b_hbm.1, s32[1,4]{1,0:T(1,128)} %bitcast.6, s32[3,8]{1,0:T(4,128)} %bitcast.5, s32[4,3]{1,0:T(4,128)} %keep_hbm.1, s32[1,12]{1,0:T(1,128)} %bitcast.7), custom_call_target="tpu_custom_call" | custom-call | tf_op jit(solution)/shard_map/expand_and_move/pallas_call | solution.py:431
  93.8 0.0 copy-start
  93.8 1.8 %copy.10 = bf16[512,384]{1,0:T(8,128)(2,1)} copy(bf16[512,384]{1,0:T(8,128)(2,1)} %get-tuple-element.8) | data formatting | bytes 786432
  95.6 0.0 copy-done
  95.6 0.8 copy.11
Async XLA Ops:
  93.8 1.9 %copy-start = (bf16[8,2,128,128]{3,2,1,0:T(8,128)(2,1)S(1)}, bf16[8,2,128,128]{3,2,1,0:T(8,128)(2,1)}, u32[]{:S(2)}) copy-start(bf16[8,2,128,128]{3,2,1,0:T(8,128)(2,1)} %get-tuple-element.5) | copy-start | bytes 1572868

commit v3 on v2

--- a/solution.py
+++ b/solution.py
@@ -12,7 +12,8 @@
 EDGE = 128
 OWN, PARTNER = 0, 1
 PARTS = {"full": (0, 512), "top": (0, 256), "bot": (256, 256)}
-CHUNKS = ((0, 256), (256, 768))
+CHUNKS = ((0, 256), (256, 256), (512, 256), (768, 256))
+BY_Z = ((1,), (1, 2))
 PARTNER_READY = 12.0
 BLOCK_US, HOP_US = 2.82, 1.8
 
@@ -24,24 +25,20 @@
         came = (dz - sign, half, dx, part) if axis == "z" else (dz, half, dx - sign, part)
         msgs.append({"axis": axis, "sign": sign, "out": (dz, half, dx, part), "in": came, "level": level})
 
-    for sign in (1, -1):
-        add("x", sign, 0, OWN, 0, "full", 0)
-    for sign in (1, -1):
-        add("x", sign, 0, OWN, -sign, "top" if sign > 0 else "bot", 0)
-    for dx in (0, -1, 1, 2):
-        for step in range(4):
-            for sign in (1, -1):
-                part = "full" if step < 3 else ("top" if sign > 0 else "bot")
-                add("z", sign, -sign * step, OWN, dx, part, 2 + step)
-    for step in range(4):
-        for sign in (1, -1):
-            part = "full" if step < 3 else ("top" if sign > 0 else "bot")
-            add("z", sign, -sign * step, PARTNER, 0, part, 1)
-    for dz in (0, -1, 1, -2, 2, -3, 3, 4):
-        for sign in (1, -1):
-            add("x", sign, dz, PARTNER, 0, "full", 1)
-        for sign in (1, -1):
-            add("x", sign, dz, PARTNER, -sign, "top" if sign > 0 else "bot", 1)
+    for half in (OWN, PARTNER):
+        for dx in (0, -1, 1, 2):
+            for step in range(4):
+                for sign in (1, -1):
+                    if dx == 0 or step + 1 in BY_Z[half]:
+                        part = "full" if step < 3 else ("top" if sign > 0 else "bot")
+                        level = (0 if dx == 0 else 2) + step * 0.1
+                        add("z", sign, -sign * step, half, dx, part, level)
+        for dz in (0, -1, 1, -2, 2, -3, 3, 4):
+            if abs(dz) not in BY_Z[half]:
+                for sign in (1, -1):
+                    add("x", sign, dz, half, 0, "full", abs(dz) * 0.1 + 0.5)
+                for sign in (1, -1):
+                    add("x", sign, dz, half, -sign, "top" if sign > 0 else "bot", abs(dz) * 0.1)
     return msgs
 
 
@@ -49,6 +46,10 @@
     dz, half, dx, part = block
     key = (dz % 8, half, dx % 4)
     return {key + ("top",), key + ("bot",)} if part == "full" else {key + (part,)}
+
+
+def group_of(m):
+    return m["in"][0] % 8, m["in"][1]
 
 
 def plan(msgs):
@@ -106,7 +107,7 @@
     groups = {}
     for k, m in enumerate(msgs):
         if k not in relayed:
-            groups.setdefault((m["in"][0] % 8, m["in"][1]), []).append(k)
+            groups.setdefault(group_of(m), []).append(k)
     for g, members in groups.items():
         steps.append((max(arrived[k] for k in members), "group", g))
     steps.sort(key=lambda e: e[0])
@@ -172,13 +173,14 @@
         m = msgs[k]
         to = col_at(m["sign"], 0, OWN) if m["axis"] == "z" else col_at(0, m["sign"], OWN)
         return pltpu.make_async_remote_copy(
-            src_ref=block(spec), dst_ref=block(spec), send_sem=a_send.at[0], recv_sem=a_recv.at[k] if k in relayed else g_recv.at[groups.index((m["in"][0] % 8, m["in"][1]))],
+            src_ref=block(spec), dst_ref=block(spec), send_sem=a_send.at[0], recv_sem=a_recv.at[k] if k in relayed else g_recv.at[groups.index(group_of(m))],
             device_id=(row, to), device_id_type=MESH,
         )
 
     def group_arrived(g):
         dz, half = g
-        ref = a_all.at[(z + dz) % 8, yh] if half == OWN else a_all.at[(z + dz) % 8, 1 - yh, (x + 2) % 4]
+        size = sum(1 if m["in"][3] == "full" else 0.5 for k, m in enumerate(msgs) if k not in relayed and group_of(m) == g)
+        ref = a_all.at[(z + dz) % 8, yh if half == OWN else 1 - yh, pl.ds(0, int(size))]
         pltpu.make_async_remote_copy(
             src_ref=ref, dst_ref=ref, send_sem=a_send.at[0], recv_sem=g_recv.at[groups.index(g)],
             device_id=(row, col_at(1, 0, OWN)), device_id_type=MESH,
@@ -227,7 +229,7 @@
     def sibling_copy(kind, chunk, py, pc):
         return pltpu.make_async_remote_copy(
             src_ref=b_slab(py, pc, chunk), dst_ref=b_slab(py, pc, chunk),
-            send_sem=s_send.at[0], recv_sem=s_recv.at[1 if kind in (3, 6) else 0],
+            send_sem=s_send.at[0], recv_sem=s_recv.at[(2 if chunk == 3 else 1) if kind in (3, 6) else 0],
             device_id=(y * 2 + 1 - core, col), device_id_type=MESH,
         )
 
@@ -263,9 +265,10 @@
         b_own(sign, 0)
     half_copy(0).wait_recv()
     half_copy(1).start()
-    for sign in (1, -1):
-        b_own(sign, 1)
-    for chunk in range(2):
+    for chunk in range(1, 4):
+        for sign in (1, -1):
+            b_own(sign, chunk)
+    for chunk in range(4):
         sibling_copy(0, chunk, y, core).start()
     loads[4].wait()
     loads[5].wait()
@@ -288,9 +291,10 @@
 
     far = jnp.where(y == 0, 3, jnp.where(y == 3, 0, -1))
 
-    def multiply(slab):
-        left = jnp.concatenate([a_all[slab, h, k] for h in range(2) for k in range(4)], axis=1)
-        acc[...] += jnp.dot(left, b_all[slab], preferred_element_type=jnp.float32)
+    def multiply(slab, first=0, count=8):
+        left = jnp.concatenate([a_all[slab, k // 4, k % 4] for k in range(first, first + count)], axis=1)
+        right = b_all[slab, pl.ds(first * EDGE, count * EDGE), :]
+        acc[...] += jnp.dot(left, right, preferred_element_type=jnp.float32)
 
     def early(dz):
         slab = (z + dz + 8) % 8
@@ -299,30 +303,29 @@
         def _():
             multiply(slab)
 
-    def siblings_arrived(count, late):
-        ref = b_all.at[pl.ds(0, count)]
+    def siblings_arrived(ref, group):
         pltpu.make_async_remote_copy(
-            src_ref=ref, dst_ref=ref, send_sem=s_send.at[0], recv_sem=s_recv.at[late],
+            src_ref=ref, dst_ref=ref, send_sem=s_send.at[0], recv_sem=s_recv.at[group],
             device_id=(y * 2 + 1 - core, col), device_id_type=MESH,
         ).wait_recv()
 
     def early_siblings():
-        pl.when(far >= 0)(lambda: siblings_arrived(3, 0))
-        pl.when(far < 0)(lambda: siblings_arrived(4, 0))
+        pl.when(far >= 0)(lambda: siblings_arrived(b_all.at[pl.ds(0, 3)], 0))
+        pl.when(far < 0)(lambda: siblings_arrived(b_all.at[pl.ds(0, 4)], 0))
 
     acc[...] = jnp.zeros_like(acc)
 
     extra = []
     for d in range(2):
-        for chunk, late in ((0, 12.5), (1, 25.5)):
+        for chunk in range(4):
             for sign in (1, -1):
-                extra.append((17.0 * d + late, functools.partial(b_arrival, sign, d, chunk, True)))
-    for d, late in ((0, 33.0), (1, 43.5)):
-        for chunk in range(2):
+                extra.append((17.0 * d + 4.25 * chunk + 14.5, functools.partial(b_arrival, sign, d, chunk, True)))
+    for d, late in ((0, 33.0), (1, 45.5)):
+        for chunk in range(4):
             for sign in (1, -1):
                 extra.append((late, functools.partial(b_arrival, sign, d, chunk, False)))
-    extra.append((45.5, early_siblings))
-    for late, dz in ((46.0, 0), (47.0, -1), (48.0, 1), (49.0, -2), (50.0, 2), (51.0, -3), (52.0, 3), (99.0, 4)):
+    extra.append((46.3, early_siblings))
+    for late, dz in ((46.31, 0), (46.32, -1), (46.33, 1), (46.34, -3), (47.75, 3), (48.8, -2), (48.81, 2), (99.0, 4)):
         extra.append((late, functools.partial(early, dz)))
     extra.sort(key=lambda e: e[0])
     for t, what, k in steps:
@@ -334,26 +337,27 @@
             group_arrived(k)
         elif what == "partner":
             half_arrival().wait_recv()
-        elif msgs[k]["out"] != (0, OWN, 0, "full") or msgs[k]["axis"] == "z" and False:
+        elif msgs[k]["out"] != (0, OWN, 0, "full"):
             a_copy(k, msgs[k]["out"]).start()
     for _, act in extra:
         act()
 
-    for chunk in range(2):
+    def far_slabs(first, count, group):
+        def more(i, carry):
+            pl.when(i == 1)(lambda: siblings_arrived(b_all.at[0, pl.ds(0, count * EDGE)], group))
+            multiply(far * 2 + (core + i) % 2, first, count)
+            return carry
+
+        @pl.when(far >= 0)
+        def _():
+            lax.fori_loop(0, 2, more, 0)
+
+    for chunk in range(4):
         for sign in (1, -1):
             b_arrival(sign, 2, chunk, False)
-
-    @pl.when(far >= 0)
-    def _():
-        def more(i, carry):
-            @pl.when(i == 1)
-            def _():
-                siblings_arrived(1, 1)
-
-            multiply(far * 2 + (core + i) % 2)
-            return carry
-
-        lax.fori_loop(0, 2, more, 0)
+        if chunk == 2:
+            far_slabs(0, 6, 1)
+    far_slabs(6, 2, 2)
 
     for c in range(3):
         cols = pl.ds(c * EDGE, EDGE)
@@ -452,19 +456,19 @@
             pltpu.SMEM((1, 12), jnp.int32),
             pltpu.SMEM((16,), jnp.int32),
             pltpu.SMEM((16,), jnp.int32),
-            dma((1,)), dma((count,)), dma((9,)),
-            dma((1,)), dma((2, 3, 2)),
-            dma((1,)), dma((2,)),
+            dma((1,)), dma((count,)), dma((16,)),
+            dma((1,)), dma((2, 3, 4)),
+            dma((1,)), dma((3,)),
             dma((2,)),
             dma((1,)), dma((1,)),
             dma((1,)), dma((1,)),
             dma((6,)),
         ],
         compiler_params=pltpu.CompilerParams(
-            collective_id=0, has_side_effects=True, vmem_limit_bytes=67043328
+            collective_id=0, has_side_effects=True, vmem_limit_bytes=40 * 1024 * 1024
         ),
         name="expand_and_move",
-    )(a, b, a_support.T, b_support.T, keep, bands.reshape(1, 12))
+    )(*(pltpu.with_memory_space_constraint(v, pltpu.HBM) for v in (a, b, a_support.T, b_support.T, keep, bands.reshape(1, 12))))
     return out, moved.reshape(2048, EDGE)
 
 

time: 96.6 us -> 94 us (0.973)
  Pallas kernels: 93.1 us -> 91.7 us
  local copies, waits for them, and re-layouts: 2.64 us -> 1.54 us
    pallas_call x1, Pallas kernels: 93.1 us -> 91.7 us  [body(): pl.pallas_call(kernel, out_shape=(jax.ShapeDtypeStruct((512, 384), jnp.bf...]
    unnamed x4 -> x2, local copies, waits for them, and re-layouts: 2.64 us -> 1.54 us
where the time goes in v3:
time: 94 us; the launch traced here: 93.9 us
  Pallas kernels  91.7 us (98%)
  local copies, waits for them, and re-layouts  1.54 us (2%)
    pallas_call x1, Pallas kernels, body(): pl.pallas_call(kernel, out_shape=(jax.ShapeDtypeStruct((512, 384), jnp.bf...  91.7 us

profile of v3, /device:TPU:1, one launch (start us, length us, event | category | flops | bytes accessed | tf_op | source)
XLA Modules:
  0.0 93.9 jit_solution(7901552065162507977)
XLA Ops:
  0.6 91.7 %expand_and_move.1 = (bf16[512,384]{1,0:T(8,128)(2,1)S(1)}, bf16[8,2,128,128]{3,2,1,0:T(8,128)(2,1)S(1)}) custom-call(bf16[512,128]{1,0:T(8,128)(2,1)} %a_hbm.1, bf16[1024,384]{1,0:T(8,128)(2,1)} %b_hbm.1, s32[1,4]{1,0:T(1,128)} %bitcast.6, s32[3,8]{1,0:T(4,128)} %bitcast.5, s32[4,3]{1,0:T(4,128)} %keep_hbm.1, s32[1,12]{1,0:T(1,128)} %bitcast.7), custom_call_target="tpu_custom_call" | custom-call | tf_op jit(solution)/shard_map/expand_and_move/pallas_call | solution.py:435
  92.3 0.7 copy.10
  93.1 0.8 copy.11

commit v4 on v3

--- a/solution.py
+++ b/solution.py
@@ -117,8 +117,8 @@
 def kernel(
     a_hbm, b_hbm, asup_hbm, bsup_hbm, keep_hbm, band_hbm,
     out_ref, moved_ref,
-    a_all, b_all, acc, tiles, outgoing, sums, relay, a_in, b_in,
-    asup_ref, bsup_ref, keep_ref, band_ref, slot_of, filled,
+    a_all, b_all, acc, tiles, slots, scales, outgoing, sums, relay, a_in, b_in,
+    asup_ref, bsup_ref, keep_ref, band_ref, slot_of, filled, third_of,
     a_send, a_recv, g_recv, b_send, b_recv, s_send, s_recv, h_recv, c_send, c_recv, r_send, r_recv, local_sem,
 ):
     row, col = lax.axis_index("row"), lax.axis_index("col")
@@ -287,6 +287,7 @@
             which = jnp.where(hit, t, which)
             any_of = jnp.where(hit, 1, any_of)
         slot_of[p] = which
+        third_of[p] = which % 3
         filled[p] = any_of
 
     far = jnp.where(y == 0, 3, jnp.where(y == 3, 0, -1))
@@ -366,7 +367,7 @@
             rows = pl.ds(r * EDGE, EDGE)
             tile = acc[rows, cols]
             tile = jnp.where(keep_ref[r, c] != 0, tile * tile, jnp.zeros_like(tile))
-            acc[rows, cols] = tile
+            tiles[r * 3 + c] = tile
             total = total + jnp.sum(tile, axis=0, keepdims=True)
         sums[row, :, cols] = total
 
@@ -378,6 +379,10 @@
 
     for k in range(7, 0, -1):
         sum_copy(k, row).start()
+    for p in range(16):
+        tile = tiles[slot_of[p]]
+        slots[p] = jnp.where(filled[p] != 0, tile, jnp.zeros_like(tile))
+
     all_sums = pltpu.make_async_remote_copy(
         src_ref=sums.at[pl.ds(0, 7)], dst_ref=sums.at[pl.ds(0, 7)], send_sem=c_send.at[0], recv_sem=c_recv.at[0],
         device_id=(row_peer(1), col), device_id_type=MESH,
@@ -388,26 +393,29 @@
     for i in range(1, 8):
         total = total + sums[i]
     scale = 1.0 / (total / (8 * 512) + 1e-5)
+    for c in range(3):
+        scales[c] = scale[:, c * EDGE:(c + 1) * EDGE]
+
+    def fill(dest):
+        for s in range(2):
+            p = dest * 2 + s
+            outgoing[dest, s] = (slots[p] * scales[third_of[p]]).astype(jnp.bfloat16)
+
+    def move(k, who):
+        return pltpu.make_async_remote_copy(
+            src_ref=outgoing.at[row_peer(k)], dst_ref=moved_ref.at[who], send_sem=r_send.at[0], recv_sem=r_recv.at[0],
+            device_id=(row_peer(k), col), device_id_type=MESH,
+        )
+
+    for k in range(7, 0, -1):
+        fill(row_peer(k))
+        move(k, row).start()
+    fill(row)
+    moved_ref[row] = outgoing[row]
     for r in range(4):
         for c in range(3):
-            rows, cols = pl.ds(r * EDGE, EDGE), pl.ds(c * EDGE, EDGE)
-            tile = (acc[rows, cols] * scale[:, c * EDGE:(c + 1) * EDGE]).astype(jnp.bfloat16)
-            out_ref[rows, cols] = tile
-            tiles[r * 3 + c] = tile
-
-    for p in range(16):
-        tile = tiles[slot_of[p]]
-        outgoing[p // 2, p % 2] = jnp.where(filled[p] != 0, tile, jnp.zeros_like(tile))
-
-    def move(k, who):
-        return pltpu.make_async_remote_copy(
-            src_ref=outgoing.at[row_peer(k)], dst_ref=moved_ref.at[who], send_sem=r_send.at[0], recv_sem=r_recv.at[0],
-            device_id=(row_peer(k), col), device_id_type=MESH,
-        )
-
-    for k in range(7, 0, -1):
-        move(k, row).start()
-    moved_ref[row] = outgoing[row]
+            tile = tiles[r * 3 + c] * scale[:, c * EDGE:(c + 1) * EDGE]
+            out_ref[pl.ds(r * EDGE, EDGE), pl.ds(c * EDGE, EDGE)] = tile.astype(jnp.bfloat16)
 
     def sent(ref, sem):
         pltpu.make_async_remote_copy(
@@ -444,7 +452,9 @@
             pltpu.VMEM((8, 2, 4, 512, EDGE), jnp.bfloat16),
             pltpu.VMEM((8, 1024, 384), jnp.bfloat16),
             pltpu.VMEM((512, 384), jnp.float32),
-            pltpu.VMEM((12, EDGE, EDGE), jnp.bfloat16),
+            pltpu.VMEM((12, EDGE, EDGE), jnp.float32),
+            pltpu.VMEM((16, EDGE, EDGE), jnp.float32),
+            pltpu.VMEM((3, 1, EDGE), jnp.float32),
             pltpu.VMEM((8, 2, EDGE, EDGE), jnp.bfloat16),
             pltpu.VMEM((8, 1, 384), jnp.float32),
             pltpu.VMEM((512, EDGE), jnp.bfloat16),
@@ -454,6 +464,7 @@
             pltpu.SMEM((3, 8), jnp.int32),
             pltpu.SMEM((4, 3), jnp.int32),
             pltpu.SMEM((1, 12), jnp.int32),
+            pltpu.SMEM((16,), jnp.int32),
             pltpu.SMEM((16,), jnp.int32),
             pltpu.SMEM((16,), jnp.int32),
             dma((1,)), dma((count,)), dma((16,)),

time: 94 us -> 93.8 us (level)
  no operation moved by 1% of the time
where the time goes in v4:
time: 93.8 us; the launch traced here: 93.7 us
  Pallas kernels  91.5 us (98%)
  local copies, waits for them, and re-layouts  1.54 us (2%)
    pallas_call x1, Pallas kernels, body(): pl.pallas_call(kernel, out_shape=(jax.ShapeDtypeStruct((512, 384), jnp.bf...  91.5 us

profile of v4, /device:TPU:1, one launch (start us, length us, event | category | flops | bytes accessed | tf_op | source)
XLA Modules:
  0.0 93.7 jit_solution(17483985338689304179)
XLA Ops:
  0.6 91.5 %expand_and_move.1 = (bf16[512,384]{1,0:T(8,128)(2,1)S(1)}, bf16[8,2,128,128]{3,2,1,0:T(8,128)(2,1)S(1)}) custom-call(bf16[512,128]{1,0:T(8,128)(2,1)} %a_hbm.1, bf16[1024,384]{1,0:T(8,128)(2,1)} %b_hbm.1, s32[1,4]{1,0:T(1,128)} %bitcast.6, s32[3,8]{1,0:T(4,128)} %bitcast.5, s32[4,3]{1,0:T(4,128)} %keep_hbm.1, s32[1,12]{1,0:T(1,128)} %bitcast.7), custom_call_target="tpu_custom_call" | custom-call | tf_op jit(solution)/shard_map/expand_and_move/pallas_call | solution.py:443
  92.2 0.7 copy.10
  92.9 0.8 copy.11

commit v5 on v4

--- a/solution.py
+++ b/solution.py
@@ -14,7 +14,7 @@
 PARTS = {"full": (0, 512), "top": (0, 256), "bot": (256, 256)}
 CHUNKS = ((0, 256), (256, 256), (512, 256), (768, 256))
 BY_Z = ((1,), (1, 2))
-PARTNER_READY = 12.0
+PARTNER_READY = 9.0
 BLOCK_US, HOP_US = 2.82, 1.8
 
 

time: 93.8 us -> 92.2 us (0.983)
  Pallas kernels: 91.5 us -> 89.9 us
    pallas_call x1, Pallas kernels: 91.5 us -> 89.9 us  [body(): pl.pallas_call(kernel, out_shape=(jax.ShapeDtypeStruct((512, 384), jnp.bf...]
where the time goes in v5:
time: 92.2 us; the launch traced here: 92.1 us
  Pallas kernels  89.9 us (98%)
  local copies, waits for them, and re-layouts  1.54 us (2%)
    pallas_call x1, Pallas kernels, body(): pl.pallas_call(kernel, out_shape=(jax.ShapeDtypeStruct((512, 384), jnp.bf...  89.9 us

profile of v5, /device:TPU:1, one launch (start us, length us, event | category | flops | bytes accessed | tf_op | source)
XLA Modules:
  0.0 92.1 jit_solution(12014579066251228215)
XLA Ops:
  0.6 89.9 %expand_and_move.1 = (bf16[512,384]{1,0:T(8,128)(2,1)S(1)}, bf16[8,2,128,128]{3,2,1,0:T(8,128)(2,1)S(1)}) custom-call(bf16[512,128]{1,0:T(8,128)(2,1)} %a_hbm.1, bf16[1024,384]{1,0:T(8,128)(2,1)} %b_hbm.1, s32[1,4]{1,0:T(1,128)} %bitcast.6, s32[3,8]{1,0:T(4,128)} %bitcast.5, s32[4,3]{1,0:T(4,128)} %keep_hbm.1, s32[1,12]{1,0:T(1,128)} %bitcast.7), custom_call_target="tpu_custom_call" | custom-call | tf_op jit(solution)/shard_map/expand_and_move/pallas_call | solution.py:443
  90.6 0.7 copy.10
  91.3 0.8 copy.11

commit v6 on v5

--- a/solution.py
+++ b/solution.py
@@ -14,7 +14,7 @@
 PARTS = {"full": (0, 512), "top": (0, 256), "bot": (256, 256)}
 CHUNKS = ((0, 256), (256, 256), (512, 256), (768, 256))
 BY_Z = ((1,), (1, 2))
-PARTNER_READY = 9.0
+PARTNER_READY = 10.0
 BLOCK_US, HOP_US = 2.82, 1.8
 
 

time: 92.2 us -> 93.4 us (1.013)
  Pallas kernels: 89.9 us -> 91.1 us
    pallas_call x1, Pallas kernels: 89.9 us -> 91.1 us  [body(): pl.pallas_call(kernel, out_shape=(jax.ShapeDtypeStruct((512, 384), jnp.bf...]
where the time goes in v6:
time: 93.4 us; the launch traced here: 93.3 us
  Pallas kernels  91.1 us (98%)
  local copies, waits for them, and re-layouts  1.54 us (2%)
    pallas_call x1, Pallas kernels, body(): pl.pallas_call(kernel, out_shape=(jax.ShapeDtypeStruct((512, 384), jnp.bf...  91.1 us

profile of v6, /device:TPU:1, one launch (start us, length us, event | category | flops | bytes accessed | tf_op | source)
XLA Modules:
  0.0 93.3 jit_solution(1217189488174971681)
XLA Ops:
  0.6 91.1 %expand_and_move.1 = (bf16[512,384]{1,0:T(8,128)(2,1)S(1)}, bf16[8,2,128,128]{3,2,1,0:T(8,128)(2,1)S(1)}) custom-call(bf16[512,128]{1,0:T(8,128)(2,1)} %a_hbm.1, bf16[1024,384]{1,0:T(8,128)(2,1)} %b_hbm.1, s32[1,4]{1,0:T(1,128)} %bitcast.6, s32[3,8]{1,0:T(4,128)} %bitcast.5, s32[4,3]{1,0:T(4,128)} %keep_hbm.1, s32[1,12]{1,0:T(1,128)} %bitcast.7), custom_call_target="tpu_custom_call" | custom-call | tf_op jit(solution)/shard_map/expand_and_move/pallas_call | solution.py:443
  91.8 0.7 copy.10
  92.5 0.8 copy.11
